TPU v7x, 128 devices: a whole 4x4x4 slice. The times are simulated.
128 devices in a mesh: expert: 16 (over y, z_lo, core), shard: 8 (over z_hi, x).
Axes of the slice: x: 4, y: 4, z: 4 (z_hi: 2, z_lo: 2; z = z_hi * 2 + z_lo), core: 2. Of those that a mesh axis runs over, the one named last changes fastest.
Arguments:
- tokens: bfloat16 [16384, 2048], P(('expert', 'shard')), may hold values from -6 to 6
- expert_ids: int32 [16384, 4], P(('expert', 'shard')), may hold values from 0 to 15, all different within a row; in each aligned block of 128 rows (0 to 127, 128 to 255, ...) at most 48 rows name the same one
- route_weights: float32 [16384, 4], P(('expert', 'shard')), may hold values from 0.1 to 1
- partner: int32 [16], replicated, may hold values from 0 to 15, as said below
- w_in: bfloat16 [16, 2, 2048, 768], P('expert', None, 'shard'), may hold values from -0.125 to 0.125
- w_down: bfloat16 [16, 768, 2048], P('expert', None, 'shard'), may hold values from -0.21875 to 0.21875
- m_in: float32 [16, 2, 2048, 768], P('expert', None, 'shard'), may hold values from -6 to 6
- v_in: float32 [16, 2, 2048, 768], P('expert', None, 'shard'), may hold values from 0.01 to 1
- m_down: float32 [16, 768, 2048], P('expert', None, 'shard'), may hold values from -6 to 6
- v_down: float32 [16, 768, 2048], P('expert', None, 'shard'), may hold values from 0.01 to 1
- cotangent: bfloat16 [16384, 2048], P(('expert', 'shard')), may hold values from -6 to 6
Outputs:
- mixed: bfloat16 [16384, 2048], P(('expert', 'shard'))
- token_grad: bfloat16 [16384, 2048], P(('expert', 'shard'))
- new_w_in: bfloat16 [16, 2, 2048, 768], P('expert', None, 'shard')
- new_w_down: bfloat16 [16, 768, 2048], P('expert', None, 'shard')
- new_m_in: float32 [16, 2, 2048, 768], P('expert', None, 'shard')
- new_v_in: float32 [16, 2, 2048, 768], P('expert', None, 'shard')
- new_m_down: float32 [16, 768, 2048], P('expert', None, 'shard')
- new_v_down: float32 [16, 768, 2048], P('expert', None, 'shard')
Inputs may be any that keep to these rules, and one draw needn't show every extreme that they name: `expert_ids`: within the rows of one device no expert is named more than 48 times, a bound that some block reaches. partner[g] is g or (g + 8) mod 16, and partner[partner[g]] = g; partner[0] is 8.
All inputs are finite; a program needn't handle non-finite values.
Results may differ from a plain program's by a relative error of at most 0.024.
Values may be sent and summed in bfloat16 or wider, within the bound.
A program may use at most 128 MiB of HBM per device.

v0:
```python
import jax
import jax.numpy as jnp
from jax import lax
from jax.sharding import PartitionSpec as P

beta_first = 0.9
beta_second = 0.999
learn_rate = 0.01
adam_eps = 1e-08
bias_first = 0.9999734386011124
bias_second = 0.09520785288629038


def shifted(block, axis, distance):
    devices = range(lax.axis_size(axis))
    route = [((i - distance) % len(devices), i) for i in devices]
    return lax.ppermute(block, axis, route)


def silu_parts(gate_pre):
    sigmoid_value = jax.nn.sigmoid(gate_pre)
    silu_value = gate_pre * sigmoid_value
    slope = sigmoid_value * (1.0 + gate_pre * (1.0 - sigmoid_value))
    return (silu_value, slope)


def adam_update(weight, first, second, grad):
    first_new = beta_first * first + (1.0 - beta_first) * grad
    second_new = beta_second * second + (1.0 - beta_second) * grad * grad
    update = learn_rate * (first_new / bias_first) / (jnp.sqrt(second_new / bias_second) + adam_eps)
    return ((weight.astype(jnp.float32) - update).astype(jnp.bfloat16), first_new, second_new)


def route_table(expert_ids, dest_rows, groups, capacity):
    entry_count = expert_ids.shape[0] * expert_ids.shape[1]
    flat_ids = expert_ids.reshape(entry_count)
    onehot = (flat_ids[:, None] == jnp.arange(groups, dtype=jnp.int32)[None, :]).astype(jnp.int32)
    before = jnp.cumsum(onehot, axis=0) - onehot
    slot_index = jnp.sum(before * onehot, axis=1)
    position = dest_rows.reshape(entry_count) * capacity + slot_index
    entry_index = jnp.arange(entry_count, dtype=jnp.int32)
    filler = jnp.full((groups * capacity,), -1, jnp.int32).at[position].set(entry_index)
    return (position, filler)


def fill_rows(source_rows, filler, groups, capacity):
    picked = jnp.take(source_rows, jnp.maximum(filler, 0), axis=0)
    kept = jnp.where((filler >= 0)[:, None], picked, jnp.zeros_like(picked))
    return kept.reshape(groups, capacity, source_rows.shape[1])


def contract_rows(left, right):
    return lax.dot_general(
        left, right, (((0,), (0,)), ((), ())), preferred_element_type=jnp.float32
    )


def contract_cols(left, right):
    return lax.dot_general(
        left, right, (((1,), (1,)), ((), ())), preferred_element_type=jnp.float32
    )


def body(
    tokens, expert_ids, route_weights, partner, w_in, w_down, m_in, v_in, m_down, v_down, cotangent
):
    groups = lax.axis_size("expert")
    halfway = groups // 2
    tok_rows = tokens.shape[0]
    width = tokens.shape[1]
    top_count = expert_ids.shape[1]
    capacity = 3 * tok_rows * top_count // (2 * groups)
    row_index = lax.axis_index("expert")
    expert_range = jnp.arange(groups, dtype=jnp.int32)
    own_partner = jnp.sum(jnp.where(expert_range == row_index, partner, 0))
    take_other = own_partner != row_index
    moved_weights = shifted((w_in, w_down), "expert", halfway)
    w_in, w_down = (
        jnp.where(take_other, moved, owned) for moved, owned in zip(moved_weights, (w_in, w_down))
    )
    moved_states = tuple(
        (
            shifted(state.astype(jnp.bfloat16), "expert", halfway).astype(state.dtype)
            for state in (m_in, v_in, m_down, v_down)
        )
    )
    m_in, v_in, m_down, v_down = (
        jnp.where(take_other, moved, owned)
        for moved, owned in zip(moved_states, (m_in, v_in, m_down, v_down))
    )
    in_full, down_full = (
        lax.all_gather(w_in, "shard", axis=2, tiled=True),
        lax.all_gather(w_down, "shard", axis=2, tiled=True),
    )
    gate_weight = in_full[0, 0]
    up_weight = in_full[0, 1]
    down_weight = down_full[0]
    hidden_width = gate_weight.shape[1]
    position, filler = route_table(expert_ids, partner[expert_ids], groups, capacity)
    token_fill = jnp.where(filler >= 0, filler // top_count, -1)
    send_rows = fill_rows(tokens, token_fill, groups, capacity)
    arrived = lax.all_to_all(send_rows, "expert", split_axis=0, concat_axis=0, tiled=True)
    rows_x = arrived.reshape(groups * capacity, width)
    own_moments = (m_in, v_in, m_down, v_down)
    gate_pre = jnp.dot(rows_x, gate_weight, preferred_element_type=jnp.float32)
    up_pre = jnp.dot(rows_x, up_weight, preferred_element_type=jnp.float32)
    silu_value, slope = silu_parts(gate_pre)
    hidden = (silu_value * up_pre).astype(jnp.bfloat16)
    expert_out = jnp.dot(hidden, down_weight, preferred_element_type=jnp.float32).astype(
        jnp.bfloat16
    )
    returned = lax.all_to_all(
        expert_out.reshape(groups, capacity, width),
        "expert",
        split_axis=0,
        concat_axis=0,
        tiled=True,
    )
    per_entry = jnp.take(returned.reshape(groups * capacity, width), position, axis=0).reshape(
        tok_rows, top_count, width
    )
    mixed = jnp.sum(route_weights[:, :, None] * per_entry.astype(jnp.float32), axis=1).astype(
        jnp.bfloat16
    )
    scaled = (route_weights[:, :, None] * cotangent[:, None, :].astype(jnp.float32)).astype(
        jnp.bfloat16
    )
    send_grads = fill_rows(scaled.reshape(tok_rows * top_count, width), filler, groups, capacity)
    dout_rows = lax.all_to_all(
        send_grads, "expert", split_axis=0, concat_axis=0, tiled=True
    ).reshape(groups * capacity, width)
    grad_hidden = contract_cols(dout_rows, down_weight)
    grad_gate = (grad_hidden * up_pre * slope).astype(jnp.bfloat16)
    grad_up = (grad_hidden * silu_value).astype(jnp.bfloat16)
    entry_grads = (
        contract_cols(grad_gate, gate_weight) + contract_cols(grad_up, up_weight)
    ).astype(jnp.bfloat16)
    back_rows = lax.all_to_all(
        entry_grads.reshape(groups, capacity, width),
        "expert",
        split_axis=0,
        concat_axis=0,
        tiled=True,
    )
    per_back = jnp.take(back_rows.reshape(groups * capacity, width), position, axis=0).reshape(
        tok_rows, top_count, width
    )
    token_grad = jnp.sum(per_back.astype(jnp.float32), axis=1).astype(jnp.bfloat16)
    grad_both = jnp.concatenate([grad_gate, grad_up], axis=1)
    share_rows = width // lax.axis_size("shard")
    shares = lax.psum_scatter(
        jnp.concatenate(
            [contract_rows(rows_x, grad_both), contract_rows(dout_rows, hidden)], axis=1
        ).astype(jnp.bfloat16),
        "shard",
        scatter_dimension=0,
        tiled=True,
    ).astype(jnp.float32)
    grad_in = jnp.transpose(
        shares[:, : 2 * hidden_width].reshape(share_rows, 2, hidden_width), (1, 0, 2)
    )[None]
    grad_down = jnp.transpose(shares[:, 2 * hidden_width :])[None]
    new_in, first_in, second_in = adam_update(w_in, own_moments[0], own_moments[1], grad_in)
    new_down, first_down, second_down = adam_update(
        w_down, own_moments[2], own_moments[3], grad_down
    )
    return (mixed, token_grad, new_in, new_down, first_in, second_in, first_down, second_down)


def solution(mesh):
    placed = (
        P(("expert", "shard"), None),
        P(("expert", "shard"), None),
        P(("expert", "shard"), None),
        P(),
        P("expert", None, "shard", None),
        P("expert", None, "shard"),
        P("expert", None, "shard", None),
        P("expert", None, "shard", None),
        P("expert", None, "shard"),
        P("expert", None, "shard"),
        P(("expert", "shard"), None),
    )
    return jax.shard_map(
        body,
        mesh=mesh,
        in_specs=placed,
        out_specs=(
            P(("expert", "shard"), None),
            P(("expert", "shard"), None),
            P("expert", None, "shard", None),
            P("expert", None, "shard"),
            P("expert", None, "shard", None),
            P("expert", None, "shard", None),
            P("expert", None, "shard"),
            P("expert", None, "shard"),
        ),
        check_vma=False,
    )
```

profile of v0, /device:TPU:1, one launch (start us, length us, event | category | flops | bytes accessed | tf_op | source)
XLA Modules:
  0.0 460.8 jit_solution(10623074164776586844)
XLA Ops:
  7.2 3.8 collective-permute-start.1
  13.0 6.8 %collective-permute-done.1 = bf16[1,768,256]{2,1,0:T(8,128)(2,1)S(1)} collective-permute-done((bf16[1,768,256]{2,1,0:T(8,128)(2,1)}, bf16[1,768,256]{2,1,0:T(8,128)(2,1)S(1)}, u32[]{:S(2)}, u32[]{:S(2)}) %collective-permute-start.1) | collective-permute-done | bytes 393248 | tf_op jit(solution)/shard_map/ppermute | solution.py:17
  23.7 16.4 %collective-permute-done = bf16[1,2,256,768]{3,2,1,0:T(8,128)(2,1)S(1)} collective-permute-done((bf16[1,2,256,768]{3,2,1,0:T(8,128)(2,1)}, bf16[1,2,256,768]{3,2,1,0:T(8,128)(2,1)S(1)}, u32[]{:S(2)}, u32[]{:S(2)}) %collective-permute-start) | collective-permute-done | bytes 786464 | tf_op jit(solution)/shard_map/ppermute | solution.py:17
  44.5 5.3 %mul.161 = f32[512,2048]{1,0:T(8,128)} reshape(f32[128,4,2048]{2,1,0:T(4,128)} %mul.160) | data formatting | bytes 8388608 | tf_op jit(solution)/shard_map/mul | solution.py:125
  50.8 10.2 %select_multiply_fusion = s32[128,4]{0,1:T(4,128)S(1)} fusion(s32[128,4]{0,1:T(4,128)S(1)} %copy-done.14, s32[]{:T(128)} %bitcast, s32[]{:T(128)} %bitcast.1, s32[]{:T(128)} %bitcast.2, s32[]{:T(128)} %bitcast.3, s32[]{:T(128)} %bitcast.4, s32[]{:T(128)} %bitcast.5, s32[]{:T(128)} %bitcast.6, s32[]{:T(128)} %bitcast.7, s32[]{:T(128)} %bitcast.8, s32[]{:T(128)} %bitcast.9, ...), kind=kLoop, calls=%fused_computation.69 | loop fusion | flops 17408 | bytes 4160 | tf_op jit(solution)/shard_map/mul | solution.py:40
  67.9 4.3 gather_fusion.1
  75.5 9.0 %all-to-all-start.2 = ((bf16[16,48,2048]{2,1,0:T(8,128)(2,1)}), bf16[16,48,2048]{2,1,0:T(8,128)(2,1)}, u32[]{:S(2)}, u32[]{:S(2)}) async-start(bf16[16,48,2048]{2,1,0:T(8,128)(2,1)} %select_select_fusion), calls=%async_computation.2 | async-start | bytes 6291456 | tf_op jit(solution)/shard_map/all_to_all | solution.py:129
  84.7 4.3 gather_fusion
  92.4 32.1 %all-to-all-done.2 = bf16[16,48,2048]{2,1,0:T(8,128)(2,1)} async-done(((bf16[16,48,2048]{2,1,0:T(8,128)(2,1)}), bf16[16,48,2048]{2,1,0:T(8,128)(2,1)}, u32[]{:S(2)}, u32[]{:S(2)}) %all-to-all-start.2) | async-done | bytes 3145760 | tf_op jit(solution)/shard_map/all_to_all | solution.py:129
  124.6 8.0 %all-to-all-start = ((bf16[16,48,2048]{2,1,0:T(8,128)(2,1)}), bf16[16,48,2048]{2,1,0:T(8,128)(2,1)S(1)}, u32[]{:S(2)}, u32[]{:S(2)}) async-start(bf16[16,48,2048]{2,1,0:T(8,128)(2,1)} %select_select_fusion.1), calls=%async_computation | async-start | bytes 6291456 | tf_op jit(solution)/shard_map/all_to_all | solution.py:102
  133.0 7.0 %fusion = f32[768,768]{0,1:T(8,128)} fusion(bf16[768,2048]{1,0:T(8,128)(2,1)} %bitcast.27, bf16[1,768,2048]{2,1,0:T(8,128)(2,1)} %all-gather.5.cloned.1.call-done), kind=kOutput, calls=%fused_computation.14 | convolution fusion | flops 2415919104 | bytes 8650752 | tf_op jit(solution)/shard_map/dot_general | solution.py:59
  140.0 32.7 %all-to-all-done = bf16[16,48,2048]{2,1,0:T(8,128)(2,1)S(1)} async-done(((bf16[16,48,2048]{2,1,0:T(8,128)(2,1)}), bf16[16,48,2048]{2,1,0:T(8,128)(2,1)S(1)}, u32[]{:S(2)}, u32[]{:S(2)}) %all-to-all-start) | async-done | bytes 3145760 | tf_op jit(solution)/shard_map/all_to_all | solution.py:102
  172.7 46.9 %all-gather.3.cloned.1.call-done = bf16[1,2,2048,768]{3,2,1,0:T(8,128)(2,1)} async-done(((bf16[1,2,256,768]{3,2,1,0:T(8,128)(2,1)}), bf16[1,2,2048,768]{3,2,1,0:T(8,128)(2,1)}) %all-gather.3.cloned.1.call-update) | async-done | bytes 6291472 | tf_op jit(solution)/shard_map/all_gather | solution.py:92
  219.6 4.7 %fusion.5 = f32[768,768]{0,1:T(8,128)S(1)} fusion(bf16[768,2048]{1,0:T(8,128)(2,1)S(1)} %bitcast.106, bf16[1,2,2048,768]{3,2,1,0:T(8,128)(2,1)} %all-gather.3.cloned.1.call-done), kind=kOutput, calls=%fused_computation.21 | convolution fusion | flops 2415919104 | bytes 8650752 | tf_op jit(solution)/shard_map/dot_general | solution.py:106
  224.3 3.5 multiply_convert_fusion.2
  227.8 5.9 %convolution_convert_fusion.1 = bf16[2048,768]{0,1:T(8,128)(2,1)S(1)} fusion(bf16[768,768]{0,1:T(8,128)(2,1)S(1)} %get-tuple-element.19, bf16[768,2048]{1,0:T(8,128)(2,1)} %bitcast.27), kind=kOutput, calls=%fused_computation.10 | convolution fusion | flops 2417491968 | bytes 7471104 | tf_op jit(solution)/shard_map/dot_general | solution.py:53
  233.8 6.3 %convolution_convert_fusion = bf16[2048,1536]{0,1:T(8,128)(2,1)S(1)} fusion(bf16[768,2048]{1,0:T(8,128)(2,1)S(1)} %bitcast.108, bf16[768,768]{0,1:T(8,128)(2,1)S(1)} %get-tuple-element.18, bf16[768,768]{0,1:T(8,128)(2,1)S(1)} %get-tuple-element.17), kind=kOutput, calls=%fused_computation.6 | convolution fusion | flops 4839702528 | bytes 11796480 | tf_op jit(solution)/shard_map/dot_general | solution.py:53
  240.1 11.6 %pad_maximum_fusion = bf16[2048,2304]{0,1:T(8,128)(2,1)} fusion(bf16[2048,768]{0,1:T(8,128)(2,1)S(1)} %convolution_convert_fusion.1, bf16[2048,1536]{0,1:T(8,128)(2,1)S(1)} %convolution_convert_fusion), kind=kLoop, calls=%fused_computation.5 | loop fusion | flops 18874368 | bytes 18874368 | tf_op jit(solution)/shard_map/concatenate | solution.py:152
  251.7 5.1 %fusion.4 = f32[768,2048]{1,0:T(8,128)S(1)} fusion(bf16[768,768]{0,1:T(8,128)(2,1)} %copy-done.17, bf16[1,2,2048,768]{3,2,1,0:T(8,128)(2,1)} %all-gather.3.cloned.1.call-done), kind=kOutput, calls=%fused_computation.20 | convolution fusion | flops 2415919104 | bytes 10616832 | tf_op jit(solution)/shard_map/dot_general | solution.py:59
  256.8 4.1 add_convert_fusion
  261.0 5.7 %all-to-all-start.3 = ((bf16[16,48,2048]{2,1,0:T(8,128)(2,1)}), bf16[16,48,2048]{2,1,0:T(8,128)(2,1)S(1)}, u32[]{:S(2)}, u32[]{:S(2)}) async-start(bf16[16,48,2048]{2,1,0:T(8,128)(2,1)} %bitcast.109), calls=%async_computation.3 | async-start | bytes 6291456 | tf_op jit(solution)/shard_map/all_to_all | solution.py:138
  266.7 6.6 %convolution_convert_fusion.2 = bf16[768,2048]{1,0:T(8,128)(2,1)} fusion(bf16[768,768]{0,1:T(8,128)(2,1)} %copy-done.19, bf16[1,768,2048]{2,1,0:T(8,128)(2,1)} %all-gather.5.cloned.1.call-done), kind=kOutput, calls=%fused_computation.11 | convolution fusion | flops 2417491968 | bytes 7471104 | tf_op jit(solution)/shard_map/dot_general | solution.py:109
  273.3 33.9 %all-to-all-done.3 = bf16[16,48,2048]{2,1,0:T(8,128)(2,1)S(1)} async-done(((bf16[16,48,2048]{2,1,0:T(8,128)(2,1)}), bf16[16,48,2048]{2,1,0:T(8,128)(2,1)S(1)}, u32[]{:S(2)}, u32[]{:S(2)}) %all-to-all-start.3) | async-done | bytes 3145760 | tf_op jit(solution)/shard_map/all_to_all | solution.py:138
  307.2 7.2 %all-to-all-start.1 = ((bf16[16,48,2048]{2,1,0:T(8,128)(2,1)}), bf16[16,48,2048]{2,1,0:T(8,128)(2,1)}, u32[]{:S(2)}, u32[]{:S(2)}) async-start(bf16[16,48,2048]{2,1,0:T(8,128)(2,1)} %bitcast.105), calls=%async_computation.1 | async-start | bytes 6291456 | tf_op jit(solution)/shard_map/all_to_all | solution.py:112
  328.9 30.2 %all-to-all-done.1 = bf16[16,48,2048]{2,1,0:T(8,128)(2,1)} async-done(((bf16[16,48,2048]{2,1,0:T(8,128)(2,1)}), bf16[16,48,2048]{2,1,0:T(8,128)(2,1)}, u32[]{:S(2)}, u32[]{:S(2)}) %all-to-all-start.1) | async-done | bytes 3145760 | tf_op jit(solution)/shard_map/all_to_all | solution.py:112
  359.1 7.7 %gather_fusion.2 = bf16[512,2048]{1,0:T(8,128)(2,1)} fusion(bf16[768,2048]{1,0:T(8,128)(2,1)} %bitcast.25, s32[1024]{0:T(1024)S(1)} %pad_clamp_fusion.1), kind=kCustom, calls=%fused_computation.clone | custom fusion | bytes 4196352 | tf_op jit(solution)/shard_map/jit(_take)/gather | solution.py:119
  366.8 4.9 %broadcast_select_fusion = (bf16[512,2048]{1,0:T(8,128)(2,1)}, f32[512,2048]{1,0:T(8,128)}) fusion(bf16[512,2048]{1,0:T(8,128)(2,1)S(1)} %copy-done.2, pred[512]{0:T(512)(128)(4,1)S(1)} %get-tuple-element.15, bf16[512,2048]{1,0:T(8,128)(2,1)} %gather_fusion.2), kind=kLoop, calls=%fused_computation.32 | loop fusion | flops 3145728 | bytes 10486272 | tf_op jit(solution)/shard_map/jit(_take)/select_n | solution.py:145
  371.7 5.2 %reshape.153 = f32[128,4,2048]{2,1,0:T(4,128)} reshape(f32[512,2048]{1,0:T(8,128)} %get-tuple-element.27) | data formatting | bytes 8388608 | tf_op jit(solution)/shard_map/convert_element_type | solution.py:122
  379.8 3.9 reduce_sum.45
  383.7 6.2 %multiply_reduce_fusion = bf16[128,2048]{1,0:T(8,128)(2,1)} fusion(f32[128,4,2048]{2,1,0:T(4,128)} %reshape.153, f32[128,4]{1,0:T(8,128)S(1)} %copy.21), kind=kLoop, calls=%fused_computation.9 | loop fusion | flops 1835008 | bytes 4720640 | tf_op jit(solution)/shard_map/reduce_sum | solution.py:122
  389.9 52.0 %reduce-scatter.2.cloned.1.call-done = bf16[256,2304]{0,1:T(8,128)(2,1)} async-done(((bf16[2048,2304]{0,1:T(8,128)(2,1)}), bf16[256,2304]{0,1:T(8,128)(2,1)}) %reduce-scatter.2.cloned.1.call-update) | async-done | bytes 1179664 | tf_op jit(solution)/shard_map/reduce_scatter | solution.py:151
  446.4 4.7 %subtract_convert_fusion = (bf16[1,2,256,768]{3,2,1,0:T(8,128)(2,1)}, f32[1,2,256,768]{3,2,1,0:T(8,128)}, f32[1,2,256,768]{3,2,1,0:T(8,128)}) fusion(bf16[1,2,256,768]{3,2,1,0:T(8,128)(2,1)S(1)} %copy-done.3, f32[256,2,768]{2,0,1:T(8,128)} %copy.28, f32[1,2,256,768]{3,2,1,0:T(8,128)S(1)} %copy-done.5, bf16[1,2,256,768]{3,2,1,0:T(8,128)(2,1)} %collective-permute-done.2, ...), kind=kLoop, calls=%fused_computation.37 | loop fusion | flops 7077888 | bytes 11010049 | tf_op jit(solution)/shard_map/convert_element_type | solution.py:31
  (109 shorter events, 49.5 us)
Async XLA Ops:
  7.2 77.6 %copy-start = (bf16[128,2048]{1,0:T(8,128)(2,1)S(1)}, bf16[128,2048]{1,0:T(8,128)(2,1)}, u32[]{:S(2)}) copy-start(bf16[128,2048]{1,0:T(8,128)(2,1)} %param.13) | copy-start | bytes 1572868
  7.2 125.8 %all-gather.5.cloned.1.call-start = ((), (), s32[]{:S(2)}) async-start(), calls=%async_computation.6 | async-start | bytes 3538944 | tf_op jit(solution)/shard_map/all_gather | solution.py:93
  7.2 12.6 %collective-permute-start.1 = (bf16[1,768,256]{2,1,0:T(8,128)(2,1)}, bf16[1,768,256]{2,1,0:T(8,128)(2,1)S(1)}, u32[]{:S(2)}, u32[]{:S(2)}) collective-permute-start(bf16[1,768,256]{2,1,0:T(8,128)(2,1)} %param.18), channel_id=1, source_target_pairs={{64,0},{72,8},{80,16},{88,24},{96,32},{104,40},{112,48},{120,56},{... | collective-permute-start | bytes 1179656 | tf_op jit(solution)/shard_map/ppermute | solution.py:17
  13.0 28.1 %copy-start.14 = (s32[128,4]{0,1:T(4,128)S(1)}, s32[128,4]{0,1:T(4,128)}, u32[]{:S(2)}) copy-start(s32[128,4]{0,1:T(4,128)} %param.14) | copy-start | bytes 6148
  13.0 28.4 %copy-start.12 = (bf16[128,2048]{1,0:T(8,128)(2,1)S(1)}, bf16[128,2048]{1,0:T(8,128)(2,1)}, u32[]{:S(2)}) copy-start(bf16[128,2048]{1,0:T(8,128)(2,1)} %param.23) | copy-start | bytes 1572868
  20.6 198.9 %all-gather.3.cloned.1.call-start = ((), (), s32[]{:S(2)}) async-start(), calls=%async_computation.5 | async-start | bytes 7077888 | tf_op jit(solution)/shard_map/all_gather | solution.py:92
  20.7 19.4 %collective-permute-start = (bf16[1,2,256,768]{3,2,1,0:T(8,128)(2,1)}, bf16[1,2,256,768]{3,2,1,0:T(8,128)(2,1)S(1)}, u32[]{:S(2)}, u32[]{:S(2)}) collective-permute-start(bf16[1,2,256,768]{3,2,1,0:T(8,128)(2,1)} %param.17), channel_id=1, source_target_pairs={{64,0},{72,8},{80,16},{88,24},{96,32},{104,40},{112,48},{120,56},{... | collective-permute-start | bytes 2359304 | tf_op jit(solution)/shard_map/ppermute | solution.py:17
  44.5 5.3 %copy-start.15 = (f32[128,4]{0,1:T(4,128)S(1)}, f32[128,4]{0,1:T(4,128)}, u32[]{:S(2)}) copy-start(f32[128,4]{0,1:T(4,128)} %param.15) | copy-start | bytes 6148
  44.5 5.6 %copy-start.13 = (s32[16]{0:T(128)S(1)}, s32[16]{0:T(128)}, u32[]{:S(2)}) copy-start(s32[16]{0:T(128)} %param.16) | copy-start | bytes 196
  75.5 49.0 %all-to-all-start.2 = ((bf16[16,48,2048]{2,1,0:T(8,128)(2,1)}), bf16[16,48,2048]{2,1,0:T(8,128)(2,1)}, u32[]{:S(2)}, u32[]{:S(2)}) async-start(bf16[16,48,2048]{2,1,0:T(8,128)(2,1)} %select_select_fusion), calls=%async_computation.2 | async-start | bytes 6291456 | tf_op jit(solution)/shard_map/all_to_all | solution.py:129
  124.6 48.1 %all-to-all-start = ((bf16[16,48,2048]{2,1,0:T(8,128)(2,1)}), bf16[16,48,2048]{2,1,0:T(8,128)(2,1)S(1)}, u32[]{:S(2)}, u32[]{:S(2)}) async-start(bf16[16,48,2048]{2,1,0:T(8,128)(2,1)} %select_select_fusion.1), calls=%async_computation | async-start | bytes 6291456 | tf_op jit(solution)/shard_map/all_to_all | solution.py:102
  132.6 309.3 %reduce-scatter.2.cloned.1.call-start = ((), (), s32[]{:S(2)}) async-start(), calls=%async_computation.7 | async-start | bytes 10616832 | tf_op jit(solution)/shard_map/reduce_scatter | solution.py:151
  227.8 5.9 %copy-start.19 = (bf16[768,768]{0,1:T(8,128)(2,1)}, bf16[768,768]{0,1:T(8,128)(2,1)S(1)}, u32[]{:S(2)}) copy-start(bf16[768,768]{0,1:T(8,128)(2,1)S(1)} %get-tuple-element.19) | copy-start | bytes 3538948
  227.8 5.9 %copy-start.17 = (bf16[768,768]{0,1:T(8,128)(2,1)}, bf16[768,768]{0,1:T(8,128)(2,1)S(1)}, u32[]{:S(2)}) copy-start(bf16[768,768]{0,1:T(8,128)(2,1)S(1)} %get-tuple-element.18) | copy-start | bytes 3538948
  227.8 5.9 %copy-start.20 = (bf16[768,768]{0,1:T(8,128)(2,1)}, bf16[768,768]{0,1:T(8,128)(2,1)S(1)}, u32[]{:S(2)}) copy-start(bf16[768,768]{0,1:T(8,128)(2,1)S(1)} %get-tuple-element.17) | copy-start | bytes 3538948
  251.7 5.1 %slice-start = ((s8[6291456]{0:T(1024)(128)(4,1)}), s8[2097152]{0:T(1024)(128)(4,1)S(1)}, s32[]{:S(2)}) async-start(s8[6291456]{0:T(1024)(128)(4,1)} %bitcast.112), calls=%async_computation.8 | async-start | bytes 4194304
  251.7 5.1 %slice-start.1 = ((s8[6291456]{0:T(1024)(128)(4,1)}), s8[4194304]{0:T(1024)(128)(4,1)S(1)}, s32[]{:S(2)}) async-start(s8[6291456]{0:T(1024)(128)(4,1)} %bitcast.112), calls=%async_computation.9 | async-start | bytes 8388608
  251.7 5.1 %copy-start.21 = (bf16[768,768]{0,1:T(8,128)(2,1)S(1)}, bf16[768,768]{0,1:T(8,128)(2,1)}, u32[]{:S(2)}) copy-start(bf16[768,768]{0,1:T(8,128)(2,1)} %copy-done.20) | copy-start | bytes 3538948
  261.0 46.3 %all-to-all-start.3 = ((bf16[16,48,2048]{2,1,0:T(8,128)(2,1)}), bf16[16,48,2048]{2,1,0:T(8,128)(2,1)S(1)}, u32[]{:S(2)}, u32[]{:S(2)}) async-start(bf16[16,48,2048]{2,1,0:T(8,128)(2,1)} %bitcast.109), calls=%async_computation.3 | async-start | bytes 6291456 | tf_op jit(solution)/shard_map/all_to_all | solution.py:138
  307.2 51.9 %all-to-all-start.1 = ((bf16[16,48,2048]{2,1,0:T(8,128)(2,1)}), bf16[16,48,2048]{2,1,0:T(8,128)(2,1)}, u32[]{:S(2)}, u32[]{:S(2)}) async-start(bf16[16,48,2048]{2,1,0:T(8,128)(2,1)} %bitcast.105), calls=%async_computation.1 | async-start | bytes 6291456 | tf_op jit(solution)/shard_map/all_to_all | solution.py:112
  314.4 5.4 %copy-start.6 = (f32[1,2,256,768]{3,2,1,0:T(8,128)S(1)}, f32[1,2,256,768]{3,2,1,0:T(8,128)}, u32[]{:S(2)}) copy-start(f32[1,2,256,768]{3,2,1,0:T(8,128)} %param.20) | copy-start | bytes 4718596
  314.4 6.5 %copy-start.8 = (f32[1,768,256]{2,1,0:T(8,128)S(1)}, f32[1,768,256]{2,1,0:T(8,128)}, u32[]{:S(2)}) copy-start(f32[1,768,256]{2,1,0:T(8,128)} %param.21) | copy-start | bytes 2359300
  314.5 10.2 %copy-start.10 = (f32[1,768,256]{2,1,0:T(8,128)S(1)}, f32[1,768,256]{2,1,0:T(8,128)}, u32[]{:S(2)}) copy-start(f32[1,768,256]{2,1,0:T(8,128)} %param.22) | copy-start | bytes 2359300
  317.0 128.0 %collective-permute-start.2 = (bf16[1,2,256,768]{3,2,1,0:T(8,128)(2,1)}, bf16[1,2,256,768]{3,2,1,0:T(8,128)(2,1)}, u32[]{:S(2)}, u32[]{:S(2)}) collective-permute-start(bf16[1,2,256,768]{3,2,1,0:T(8,128)(2,1)} %convert_element_type.94), channel_id=1, source_target_pairs={{64,0},{72,8},{80,16},{88,24},{96,32},{104,40},{112,48},{120,56},{... | collective-permute-start | bytes 2359304 | tf_op jit(solution)/shard_map/ppermute | solution.py:17
  320.8 124.2 %collective-permute-start.3 = (bf16[1,2,256,768]{3,2,1,0:T(8,128)(2,1)}, bf16[1,2,256,768]{3,2,1,0:T(8,128)(2,1)}, u32[]{:S(2)}, u32[]{:S(2)}) collective-permute-start(bf16[1,2,256,768]{3,2,1,0:T(8,128)(2,1)} %convert_element_type.97), channel_id=1, source_target_pairs={{64,0},{72,8},{80,16},{88,24},{96,32},{104,40},{112,48},{120,56},{... | collective-permute-start | bytes 2359304 | tf_op jit(solution)/shard_map/ppermute | solution.py:17
  321.8 129.4 %collective-permute-start.4 = (bf16[1,768,256]{2,1,0:T(8,128)(2,1)}, bf16[1,768,256]{2,1,0:T(8,128)(2,1)}, u32[]{:S(2)}, u32[]{:S(2)}) collective-permute-start(bf16[1,768,256]{2,1,0:T(8,128)(2,1)} %convert_element_type.101), channel_id=1, source_target_pairs={{64,0},{72,8},{80,16},{88,24},{96,32},{104,40},{112,48},{120,56},{... | collective-permute-start | bytes 1179656 | tf_op jit(solution)/shard_map/ppermute | solution.py:17
  325.4 125.8 %collective-permute-start.5 = (bf16[1,768,256]{2,1,0:T(8,128)(2,1)}, bf16[1,768,256]{2,1,0:T(8,128)(2,1)}, u32[]{:S(2)}, u32[]{:S(2)}) collective-permute-start(bf16[1,768,256]{2,1,0:T(8,128)(2,1)} %convert_element_type.103), channel_id=1, source_target_pairs={{64,0},{72,8},{80,16},{88,24},{96,32},{104,40},{112,48},{120,56},{... | collective-permute-start | bytes 1179656 | tf_op jit(solution)/shard_map/ppermute | solution.py:17
  359.1 7.7 %copy-start.2 = (bf16[512,2048]{1,0:T(8,128)(2,1)S(1)}, bf16[512,2048]{1,0:T(8,128)(2,1)}, u32[]{:S(2)}) copy-start(bf16[512,2048]{1,0:T(8,128)(2,1)} %gather_fusion.3) | copy-start | bytes 6291460
  445.0 6.2 %copy-start.7 = (bf16[1,768,256]{2,1,0:T(8,128)(2,1)S(1)}, bf16[1,768,256]{2,1,0:T(8,128)(2,1)}, u32[]{:S(2)}) copy-start(bf16[1,768,256]{2,1,0:T(8,128)(2,1)} %broadcast_select_fusion.2) | copy-start | bytes 1179652
  445.0 6.2 %copy-start.9 = (f32[1,768,256]{2,1,0:T(8,128)S(1)}, f32[1,768,256]{2,1,0:T(8,128)}, u32[]{:S(2)}) copy-start(f32[1,768,256]{2,1,0:T(8,128)} %param.21) | copy-start | bytes 2359300
  445.0 6.2 %copy-start.11 = (f32[1,768,256]{2,1,0:T(8,128)S(1)}, f32[1,768,256]{2,1,0:T(8,128)}, u32[]{:S(2)}) copy-start(f32[1,768,256]{2,1,0:T(8,128)} %param.22) | copy-start | bytes 2359300
  446.4 7.7 %copy-start.1 = (bf16[128,2048]{1,0:T(8,128)(2,1)S(1)}, bf16[128,2048]{1,0:T(8,128)(2,1)}, u32[]{:S(2)}) copy-start(bf16[128,2048]{1,0:T(8,128)(2,1)} %param.13) | copy-start | bytes 1572868
  (5 other events, 13.8 us)
Sparse Core Ops, SparseCore 0:
  20.8 70.2 all-gather.4
  93.8 125.6 all-gather.2
  251.8 190.0 reduce-scatter.1
where the time goes:
time: 467 us; the launch traced here: 461 us
  waiting for transfers between devices  251 us (54%)
  other arithmetic  63.2 us (14%)
  local copies, waits for them, and re-layouts  45 us (10%)
  matrix products  43.3 us (9%)
  starting transfers between devices  43.2 us (9%)
  between operations  15.1 us (3%)
    reduce_scatter x1, waiting for transfers between devices, body(): lax.psum_scatter(jnp.concatenate([contract_rows(rows_x, grad_both), contr...  52 us
    all_gather x1, waiting for transfers between devices, body(): lax.all_gather(w_in, 'shard', axis=2, tiled=True)  46.9 us
    all_to_all x1, waiting for transfers between devices, body(): lax.all_to_all(entry_grads.reshape(groups, capacity, width), 'expert', sp...  33.9 us
    all_to_all x1, waiting for transfers between devices, body(): lax.all_to_all(send_rows, 'expert', split_axis=0, concat_axis=0, tiled=True)  32.7 us
    all_to_all x1, waiting for transfers between devices, body(): lax.all_to_all(send_grads, 'expert', split_axis=0, concat_axis=0, tiled=T...  32.1 us
    all_to_all x1, waiting for transfers between devices, body(): lax.all_to_all(expert_out.reshape(groups, capacity, width), 'expert', spl...  30.2 us
    ppermute x6, waiting for transfers between devices, shifted(): return lax.ppermute(block, axis, route)  23.2 us
    dot_general x3, matrix products, contract_cols(): lax.dot_general(left, right, (((1,), (1,)), ((), ())), preferred_element_...  16.2 us
  transfers between devices with their start and end apart: 13, of which 8 were waited for; matrix products, arithmetic and copies ran while one was open for 25% of the time, Pallas kernels for 0%

commit v1 on v0

--- a/solution.py
+++ b/solution.py
@@ -89,7 +89,15 @@
         for moved, owned in zip(moved_states, (m_in, v_in, m_down, v_down))
     )
     in_full, down_full = (
-        lax.all_gather(w_in, "shard", axis=2, tiled=True),
+        jnp.concatenate(
+            lax.all_to_all(
+                jnp.stack([w_in for _ in range(lax.axis_size("shard"))], axis=0),
+                "shard",
+                split_axis=0,
+                concat_axis=0,
+            ),
+            2,
+        ),
         lax.all_gather(w_down, "shard", axis=2, tiled=True),
     )
     gate_weight = in_full[0, 0]

time: 467 us -> 512 us (1.096)
  waiting for transfers between devices: 251 us -> 284 us
  local copies, waits for them, and re-layouts: 45 us -> 53.9 us
    all_to_all x0 -> x1, waiting for transfers between devices: none -> 49 us  [body(): lax.all_to_all(jnp.stack([w_in for _ in range(lax.axis_size('shard'))], a...]
    all_gather x1 -> x0, waiting for transfers between devices: 46.9 us -> none  [body(): lax.all_gather(w_in, 'shard', axis=2, tiled=True)]
    ppermute x6, waiting for transfers between devices: 23.2 us -> 66.7 us  [shifted(): return lax.ppermute(block, axis, route)]
    all_to_all x1, waiting for transfers between devices: 32.7 us -> 0.01 us  [body(): lax.all_to_all(send_rows, 'expert', split_axis=0, concat_axis=0, tiled=True)]
    all_gather x1, waiting for transfers between devices: 0.02 us -> 19.3 us  [body(): lax.all_gather(w_down, 'shard', axis=2, tiled=True)]
    all_to_all x0 -> x1, starting transfers between devices: none -> 7.17 us  [body(): lax.all_to_all(jnp.stack([w_in for _ in range(lax.axis_size('shard'))], a...]
    all_to_all x1, waiting for transfers between devices: 32.1 us -> 26.3 us  [body(): lax.all_to_all(send_grads, 'expert', split_axis=0, concat_axis=0, tiled=T...]
    reduce_scatter x1, waiting for transfers between devices: 52 us -> 57.7 us  [body(): lax.psum_scatter(jnp.concatenate([contract_rows(rows_x, grad_both), contr...]
  transfers between devices with their start and end apart: 13 -> 13, of which waited for: 8 -> 8; matrix products, arithmetic and copies ran while one was open for 25% -> 20% of each run, Pallas kernels for 0% -> 0%
where the time goes in v1:
time: 512 us; the launch traced here: 505 us
  waiting for transfers between devices  284 us (55%)
  other arithmetic  62.7 us (12%)
  local copies, waits for them, and re-layouts  53.9 us (11%)
  matrix products  48.2 us (9%)
  starting transfers between devices  40.1 us (8%)
  between operations  15.6 us (3%)
    ppermute x6, waiting for transfers between devices, shifted(): return lax.ppermute(block, axis, route)  66.7 us
    reduce_scatter x1, waiting for transfers between devices, body(): lax.psum_scatter(jnp.concatenate([contract_rows(rows_x, grad_both), contr...  57.7 us
    all_to_all x1, waiting for transfers between devices, body(): lax.all_to_all(jnp.stack([w_in for _ in range(lax.axis_size('shard'))], a...  49 us
    all_to_all x1, waiting for transfers between devices, body(): lax.all_to_all(entry_grads.reshape(groups, capacity, width), 'expert', sp...  37.8 us
    all_to_all x1, waiting for transfers between devices, body(): lax.all_to_all(expert_out.reshape(groups, capacity, width), 'expert', spl...  27.4 us
    all_to_all x1, waiting for transfers between devices, body(): lax.all_to_all(send_grads, 'expert', split_axis=0, concat_axis=0, tiled=T...  26.3 us
    all_gather x1, waiting for transfers between devices, body(): lax.all_gather(w_down, 'shard', axis=2, tiled=True)  19.3 us
    dot_general x3, matrix products, contract_cols(): lax.dot_general(left, right, (((1,), (1,)), ((), ())), preferred_element_...  15.8 us
  transfers between devices with their start and end apart: 13, of which 8 were waited for; matrix products, arithmetic and copies ran while one was open for 20% of the time, Pallas kernels for 0%

profile of v1, /device:TPU:1, one launch (start us, length us, event | category | flops | bytes accessed | tf_op | source)
XLA Modules:
  0.0 504.8 jit_solution(12579448943334867809)
XLA Ops:
  10.2 10.8 %select_multiply_fusion = s32[128,4]{0,1:T(4,128)S(1)} fusion(s32[128,4]{0,1:T(4,128)} %param.14, s32[]{:T(128)} %bitcast, s32[]{:T(128)} %bitcast.1, s32[]{:T(128)} %bitcast.2, s32[]{:T(128)} %bitcast.3, s32[]{:T(128)} %bitcast.4, s32[]{:T(128)} %bitcast.5, s32[]{:T(128)} %bitcast.6, s32[]{:T(128)} %bitcast.7, s32[]{:T(128)} %bitcast.8, s32[]{:T(128)} %bitcast.9, ...), kind=kLoop, calls=%fused_computation.70 | loop fusion | flops 17408 | bytes 4160 | tf_op jit(solution)/shard_map/mul | solution.py:40
  25.5 4.3 gather_fusion
  33.0 7.5 %all-to-all-start = ((bf16[16,48,2048]{2,1,0:T(8,128)(2,1)}), bf16[16,48,2048]{2,1,0:T(8,128)(2,1)}, u32[]{:S(2)}, u32[]{:S(2)}) async-start(bf16[16,48,2048]{2,1,0:T(8,128)(2,1)} %select_select_fusion.1), calls=%async_computation | async-start | bytes 6291456 | tf_op jit(solution)/shard_map/all_to_all | solution.py:110
  44.8 55.6 %collective-permute-done = bf16[1,2,256,768]{3,2,1,0:T(8,128)(2,1)S(1)} collective-permute-done((bf16[1,2,256,768]{3,2,1,0:T(8,128)(2,1)S(1)}, bf16[1,2,256,768]{3,2,1,0:T(8,128)(2,1)S(1)}, u32[]{:S(2)}, u32[]{:S(2)}) %collective-permute-start) | collective-permute-done | bytes 786464 | tf_op jit(solution)/shard_map/ppermute | solution.py:17
  103.7 7.2 %all-to-all-start.1 = ((bf16[8,1,2,256,768]{4,3,2,1,0:T(8,128)(2,1)}), bf16[8,1,2,256,768]{4,3,2,1,0:T(8,128)(2,1)}, u32[]{:S(2)}, u32[]{:S(2)}) async-start(bf16[8,1,2,256,768]{4,3,2,1,0:T(8,128)(2,1)} %stack.2), calls=%async_computation.1 | async-start | bytes 12582912 | tf_op jit(solution)/shard_map/all_to_all | solution.py:93
  111.1 11.1 %collective-permute-done.1 = bf16[1,768,256]{2,1,0:T(8,128)(2,1)S(1)} collective-permute-done((bf16[1,768,256]{2,1,0:T(8,128)(2,1)S(1)}, bf16[1,768,256]{2,1,0:T(8,128)(2,1)S(1)}, u32[]{:S(2)}, u32[]{:S(2)}) %collective-permute-start.1) | collective-permute-done | bytes 393248 | tf_op jit(solution)/shard_map/ppermute | solution.py:17
  125.9 5.3 %mul.161 = f32[512,2048]{1,0:T(8,128)} reshape(f32[128,4,2048]{2,1,0:T(4,128)} %mul.160) | data formatting | bytes 8388608 | tf_op jit(solution)/shard_map/mul | solution.py:133
  134.1 4.3 gather_fusion.1
  141.8 49.0 %all-to-all-done.1 = bf16[8,1,2,256,768]{4,3,2,1,0:T(8,128)(2,1)} async-done(((bf16[8,1,2,256,768]{4,3,2,1,0:T(8,128)(2,1)}), bf16[8,1,2,256,768]{4,3,2,1,0:T(8,128)(2,1)}, u32[]{:S(2)}, u32[]{:S(2)}) %all-to-all-start.1) | async-done | bytes 6291488 | tf_op jit(solution)/shard_map/all_to_all | solution.py:93
  190.8 4.4 all-to-all-start.3
  195.7 3.4 copy.35
  199.1 8.4 %fusion.4 = f32[768,768]{0,1:T(8,128)} fusion(bf16[768,2048]{1,0:T(8,128)(2,1)} %bitcast.20, bf16[1,2,2048,768]{3,2,1,0:T(8,128)(2,1)S(1)} %bitcast.109), kind=kOutput, calls=%fused_computation.20 | convolution fusion | flops 2415919104 | bytes 8650752 | tf_op jit(solution)/shard_map/dot_general | solution.py:113
  207.5 6.1 %fusion.5 = f32[768,768]{0,1:T(8,128)} fusion(bf16[768,2048]{1,0:T(8,128)(2,1)} %bitcast.20, bf16[1,2,2048,768]{3,2,1,0:T(8,128)(2,1)S(1)} %bitcast.110), kind=kOutput, calls=%fused_computation.21 | convolution fusion | flops 2415919104 | bytes 8650752 | tf_op jit(solution)/shard_map/dot_general | solution.py:114
  213.6 26.3 %all-to-all-done.3 = bf16[16,48,2048]{2,1,0:T(8,128)(2,1)S(1)} async-done(((bf16[16,48,2048]{2,1,0:T(8,128)(2,1)}), bf16[16,48,2048]{2,1,0:T(8,128)(2,1)S(1)}, u32[]{:S(2)}, u32[]{:S(2)}) %all-to-all-start.3) | async-done | bytes 3145760 | tf_op jit(solution)/shard_map/all_to_all | solution.py:137
  239.9 19.3 %all-gather.2.cloned.1.call-done = bf16[1,768,2048]{2,1,0:T(8,128)(2,1)} async-done(((bf16[1,768,256]{2,1,0:T(8,128)(2,1)}), bf16[1,768,2048]{2,1,0:T(8,128)(2,1)}) %all-gather.2.cloned.1.call-update) | async-done | bytes 3145744 | tf_op jit(solution)/shard_map/all_gather | solution.py:101
  259.2 6.7 %multiply_convert_fusion.1 = (bf16[768,768]{0,1:T(8,128)(2,1)S(1)}, bf16[768,768]{0,1:T(8,128)(2,1)S(1)}, bf16[768,768]{0,1:T(8,128)(2,1)S(1)}) fusion(f32[768,768]{0,1:T(8,128)} %fusion.4, f32[768,768]{0,1:T(8,128)} %fusion.5, bf16[768,2048]{1,0:T(8,128)(2,1)S(1)} %bitcast.117, bf16[1,768,2048]{2,1,0:T(8,128)(2,1)} %all-gather.2.cloned.1.call-done), kind=kOutput, calls=%fused_computation.26 | convolution fusion | flops 2424766464 | bytes 14548992 | tf_op jit(solution)/shard_map/dot_general | solution.py:59
  268.9 8.3 %convolution_convert_fusion = bf16[2048,1536]{0,1:T(8,128)(2,1)S(1)} fusion(bf16[768,2048]{1,0:T(8,128)(2,1)} %bitcast.20, bf16[768,768]{0,1:T(8,128)(2,1)S(1)} %get-tuple-element.17, bf16[768,768]{0,1:T(8,128)(2,1)S(1)} %get-tuple-element.18), kind=kOutput, calls=%fused_computation.6 | convolution fusion | flops 4839702528 | bytes 11796480 | tf_op jit(solution)/shard_map/dot_general | solution.py:53
  277.2 11.6 %pad_maximum_fusion = bf16[2048,2304]{0,1:T(8,128)(2,1)} fusion(bf16[2048,768]{0,1:T(8,128)(2,1)S(1)} %convolution_convert_fusion.1, bf16[2048,1536]{0,1:T(8,128)(2,1)S(1)} %convolution_convert_fusion), kind=kLoop, calls=%fused_computation.5 | loop fusion | flops 18874368 | bytes 18874368 | tf_op jit(solution)/shard_map/concatenate | solution.py:160
  288.9 5.1 %fusion.3 = f32[768,2048]{1,0:T(8,128)S(1)} fusion(bf16[768,768]{0,1:T(8,128)(2,1)} %copy-done.20, bf16[1,2,2048,768]{3,2,1,0:T(8,128)(2,1)} %bitcast.111), kind=kOutput, calls=%fused_computation.19 | convolution fusion | flops 2415919104 | bytes 10616832 | tf_op jit(solution)/shard_map/dot_general | solution.py:59
  294.0 4.1 add_convert_fusion
  298.1 6.8 %all-to-all-start.4 = ((bf16[16,48,2048]{2,1,0:T(8,128)(2,1)}), bf16[16,48,2048]{2,1,0:T(8,128)(2,1)S(1)}, u32[]{:S(2)}, u32[]{:S(2)}) async-start(bf16[16,48,2048]{2,1,0:T(8,128)(2,1)} %bitcast.119), calls=%async_computation.4 | async-start | bytes 6291456 | tf_op jit(solution)/shard_map/all_to_all | solution.py:146
  304.9 6.6 %convolution_convert_fusion.2 = bf16[768,2048]{1,0:T(8,128)(2,1)} fusion(bf16[768,768]{0,1:T(8,128)(2,1)} %copy-done.21, bf16[1,768,2048]{2,1,0:T(8,128)(2,1)} %all-gather.2.cloned.1.call-done), kind=kOutput, calls=%fused_computation.11 | convolution fusion | flops 2417491968 | bytes 7471104 | tf_op jit(solution)/shard_map/dot_general | solution.py:117
  311.5 37.8 %all-to-all-done.4 = bf16[16,48,2048]{2,1,0:T(8,128)(2,1)S(1)} async-done(((bf16[16,48,2048]{2,1,0:T(8,128)(2,1)}), bf16[16,48,2048]{2,1,0:T(8,128)(2,1)S(1)}, u32[]{:S(2)}, u32[]{:S(2)}) %all-to-all-start.4) | async-done | bytes 3145760 | tf_op jit(solution)/shard_map/all_to_all | solution.py:146
  349.2 4.8 all-to-all-start.2
  368.5 27.4 %all-to-all-done.2 = bf16[16,48,2048]{2,1,0:T(8,128)(2,1)} async-done(((bf16[16,48,2048]{2,1,0:T(8,128)(2,1)}), bf16[16,48,2048]{2,1,0:T(8,128)(2,1)}, u32[]{:S(2)}, u32[]{:S(2)}) %all-to-all-start.2) | async-done | bytes 3145760 | tf_op jit(solution)/shard_map/all_to_all | solution.py:120
  395.9 7.7 %gather_fusion.2 = bf16[512,2048]{1,0:T(8,128)(2,1)} fusion(bf16[768,2048]{1,0:T(8,128)(2,1)} %bitcast.29, s32[1024]{0:T(1024)S(1)} %pad_clamp_fusion.1), kind=kCustom, calls=%fused_computation.clone | custom fusion | bytes 4196352 | tf_op jit(solution)/shard_map/jit(_take)/gather | solution.py:127
  403.6 4.8 broadcast_select_fusion
  408.4 5.3 %reshape.164 = f32[128,4,2048]{2,1,0:T(4,128)} reshape(f32[512,2048]{1,0:T(8,128)} %get-tuple-element.27) | data formatting | bytes 8388608 | tf_op jit(solution)/shard_map/convert_element_type | solution.py:130
  416.7 3.9 reduce_sum.45
  420.6 6.2 %multiply_reduce_fusion = bf16[128,2048]{1,0:T(8,128)(2,1)} fusion(f32[128,4,2048]{2,1,0:T(4,128)} %reshape.164, f32[128,4]{1,0:T(8,128)S(1)} %copy.29), kind=kLoop, calls=%fused_computation.9 | loop fusion | flops 1835008 | bytes 4720640 | tf_op jit(solution)/shard_map/reduce_sum | solution.py:130
  426.8 57.7 %reduce-scatter.2.cloned.1.call-done = bf16[256,2304]{0,1:T(8,128)(2,1)} async-done(((bf16[2048,2304]{0,1:T(8,128)(2,1)}), bf16[256,2304]{0,1:T(8,128)(2,1)}) %reduce-scatter.2.cloned.1.call-update) | async-done | bytes 1179664 | tf_op jit(solution)/shard_map/reduce_scatter | solution.py:159
  489.3 5.2 %subtract_convert_fusion = (bf16[1,2,256,768]{3,2,1,0:T(8,128)(2,1)}, f32[1,2,256,768]{3,2,1,0:T(8,128)}, f32[1,2,256,768]{3,2,1,0:T(8,128)}) fusion(bf16[1,2,256,768]{3,2,1,0:T(8,128)(2,1)} %copy-done.11, bf16[1,2,256,768]{3,2,1,0:T(8,128)(2,1)S(1)} %copy-done.10, pred[]{:T(512)S(6)} %ne.20, f32[256,2,768]{2,0,1:T(8,128)} %copy.37, ...), kind=kLoop, calls=%fused_computation.37 | loop fusion | flops 7471104 | bytes 11796481 | tf_op jit(solution)/shard_map/convert_element_type | solution.py:31
  (114 shorter events, 56.5 us)
Async XLA Ops:
  7.2 18.3 %copy-start = (bf16[128,2048]{1,0:T(8,128)(2,1)S(1)}, bf16[128,2048]{1,0:T(8,128)(2,1)}, u32[]{:S(2)}) copy-start(bf16[128,2048]{1,0:T(8,128)(2,1)} %param.13) | copy-start | bytes 1572868
  33.0 7.5 %copy-start.9 = (bf16[1,2,256,768]{3,2,1,0:T(8,128)(2,1)S(1)}, bf16[1,2,256,768]{3,2,1,0:T(8,128)(2,1)}, u32[]{:S(2)}) copy-start(bf16[1,2,256,768]{3,2,1,0:T(8,128)(2,1)} %param.17) | copy-start | bytes 2359300
  33.0 10.5 %copy-start.18 = (s32[16]{0:T(128)S(1)}, s32[16]{0:T(128)}, u32[]{:S(2)}) copy-start(s32[16]{0:T(128)} %param.16) | copy-start | bytes 196
  33.0 67.4 %all-to-all-start = ((bf16[16,48,2048]{2,1,0:T(8,128)(2,1)}), bf16[16,48,2048]{2,1,0:T(8,128)(2,1)}, u32[]{:S(2)}, u32[]{:S(2)}) async-start(bf16[16,48,2048]{2,1,0:T(8,128)(2,1)} %select_select_fusion.1), calls=%async_computation | async-start | bytes 6291456 | tf_op jit(solution)/shard_map/all_to_all | solution.py:110
  40.5 59.9 %collective-permute-start = (bf16[1,2,256,768]{3,2,1,0:T(8,128)(2,1)S(1)}, bf16[1,2,256,768]{3,2,1,0:T(8,128)(2,1)S(1)}, u32[]{:S(2)}, u32[]{:S(2)}) collective-permute-start(bf16[1,2,256,768]{3,2,1,0:T(8,128)(2,1)S(1)} %copy-done.9), channel_id=1, source_target_pairs={{64,0},{72,8},{80,16},{88,24},{96,32},{104,40},{112,48},{120,56},{... | collective-permute-start | bytes 2359304 | tf_op jit(solution)/shard_map/ppermute | solution.py:17
  100.4 3.3 copy-start.11
  103.7 7.2 %copy-start.17 = (bf16[1,768,256]{2,1,0:T(8,128)(2,1)S(1)}, bf16[1,768,256]{2,1,0:T(8,128)(2,1)}, u32[]{:S(2)}) copy-start(bf16[1,768,256]{2,1,0:T(8,128)(2,1)} %param.18) | copy-start | bytes 1179652
  103.7 19.2 %copy-start.16 = (bf16[128,2048]{1,0:T(8,128)(2,1)S(1)}, bf16[128,2048]{1,0:T(8,128)(2,1)}, u32[]{:S(2)}) copy-start(bf16[128,2048]{1,0:T(8,128)(2,1)} %param.23) | copy-start | bytes 1572868
  103.7 87.1 %all-to-all-start.1 = ((bf16[8,1,2,256,768]{4,3,2,1,0:T(8,128)(2,1)}), bf16[8,1,2,256,768]{4,3,2,1,0:T(8,128)(2,1)}, u32[]{:S(2)}, u32[]{:S(2)}) async-start(bf16[8,1,2,256,768]{4,3,2,1,0:T(8,128)(2,1)} %stack.2), calls=%async_computation.1 | async-start | bytes 12582912 | tf_op jit(solution)/shard_map/all_to_all | solution.py:93
  110.9 148.3 %all-gather.2.cloned.1.call-start = ((), (), s32[]{:S(2)}) async-start(), calls=%async_computation.6 | async-start | bytes 3538944 | tf_op jit(solution)/shard_map/all_gather | solution.py:101
  111.0 11.1 %collective-permute-start.1 = (bf16[1,768,256]{2,1,0:T(8,128)(2,1)S(1)}, bf16[1,768,256]{2,1,0:T(8,128)(2,1)S(1)}, u32[]{:S(2)}, u32[]{:S(2)}) collective-permute-start(bf16[1,768,256]{2,1,0:T(8,128)(2,1)S(1)} %copy-done.17), channel_id=1, source_target_pairs={{64,0},{72,8},{80,16},{88,24},{96,32},{104,40},{112,48},{120,56},{... | collective-permute-start | bytes 1179656 | tf_op jit(solution)/shard_map/ppermute | solution.py:17
  125.9 5.3 %copy-start.19 = (f32[128,4]{0,1:T(4,128)S(1)}, f32[128,4]{0,1:T(4,128)}, u32[]{:S(2)}) copy-start(f32[128,4]{0,1:T(4,128)} %param.15) | copy-start | bytes 6148
  190.8 49.1 %all-to-all-start.3 = ((bf16[16,48,2048]{2,1,0:T(8,128)(2,1)}), bf16[16,48,2048]{2,1,0:T(8,128)(2,1)S(1)}, u32[]{:S(2)}, u32[]{:S(2)}) async-start(bf16[16,48,2048]{2,1,0:T(8,128)(2,1)} %select_select_fusion), calls=%async_computation.3 | async-start | bytes 6291456 | tf_op jit(solution)/shard_map/all_to_all | solution.py:137
  195.2 289.3 %reduce-scatter.2.cloned.1.call-start = ((), (), s32[]{:S(2)}) async-start(), calls=%async_computation.7 | async-start | bytes 10616832 | tf_op jit(solution)/shard_map/reduce_scatter | solution.py:159
  199.1 8.4 %copy-start.4 = (bf16[8,1,2,256,768]{4,3,0,2,1:T(8,128)(2,1)}, bf16[8,1,2,256,768]{4,3,0,2,1:T(8,128)(2,1)S(1)}, u32[]{:S(2)}) copy-start(bf16[8,1,2,256,768]{4,3,0,2,1:T(8,128)(2,1)S(1)} %copy.35) | copy-start | bytes 18874372
  288.8 5.1 %slice-start = ((s8[6291456]{0:T(1024)(128)(4,1)}), s8[2097152]{0:T(1024)(128)(4,1)S(1)}, s32[]{:S(2)}) async-start(s8[6291456]{0:T(1024)(128)(4,1)} %bitcast.112), calls=%async_computation.8 | async-start | bytes 4194304
  288.9 5.1 %slice-start.1 = ((s8[6291456]{0:T(1024)(128)(4,1)}), s8[4194304]{0:T(1024)(128)(4,1)S(1)}, s32[]{:S(2)}) async-start(s8[6291456]{0:T(1024)(128)(4,1)} %bitcast.112), calls=%async_computation.9 | async-start | bytes 8388608
  288.9 5.1 %copy-start.23 = (bf16[768,768]{0,1:T(8,128)(2,1)S(1)}, bf16[768,768]{0,1:T(8,128)(2,1)}, u32[]{:S(2)}) copy-start(bf16[768,768]{0,1:T(8,128)(2,1)} %copy-done.22) | copy-start | bytes 3538948
  298.1 51.2 %all-to-all-start.4 = ((bf16[16,48,2048]{2,1,0:T(8,128)(2,1)}), bf16[16,48,2048]{2,1,0:T(8,128)(2,1)S(1)}, u32[]{:S(2)}, u32[]{:S(2)}) async-start(bf16[16,48,2048]{2,1,0:T(8,128)(2,1)} %bitcast.119), calls=%async_computation.4 | async-start | bytes 6291456 | tf_op jit(solution)/shard_map/all_to_all | solution.py:146
  349.2 46.6 %all-to-all-start.2 = ((bf16[16,48,2048]{2,1,0:T(8,128)(2,1)}), bf16[16,48,2048]{2,1,0:T(8,128)(2,1)}, u32[]{:S(2)}, u32[]{:S(2)}) async-start(bf16[16,48,2048]{2,1,0:T(8,128)(2,1)} %bitcast.116), calls=%async_computation.2 | async-start | bytes 6291456 | tf_op jit(solution)/shard_map/all_to_all | solution.py:120
  354.0 5.4 %copy-start.6 = (f32[1,2,256,768]{3,2,1,0:T(8,128)S(1)}, f32[1,2,256,768]{3,2,1,0:T(8,128)}, u32[]{:S(2)}) copy-start(f32[1,2,256,768]{3,2,1,0:T(8,128)} %param.20) | copy-start | bytes 4718596
  354.0 6.5 %copy-start.12 = (f32[1,768,256]{2,1,0:T(8,128)S(1)}, f32[1,768,256]{2,1,0:T(8,128)}, u32[]{:S(2)}) copy-start(f32[1,768,256]{2,1,0:T(8,128)} %param.21) | copy-start | bytes 2359300
  354.1 10.2 %copy-start.14 = (f32[1,768,256]{2,1,0:T(8,128)S(1)}, f32[1,768,256]{2,1,0:T(8,128)}, u32[]{:S(2)}) copy-start(f32[1,768,256]{2,1,0:T(8,128)} %param.22) | copy-start | bytes 2359300
  356.6 131.1 %collective-permute-start.2 = (bf16[1,2,256,768]{3,2,1,0:T(8,128)(2,1)}, bf16[1,2,256,768]{3,2,1,0:T(8,128)(2,1)}, u32[]{:S(2)}, u32[]{:S(2)}) collective-permute-start(bf16[1,2,256,768]{3,2,1,0:T(8,128)(2,1)} %convert_element_type.94), channel_id=1, source_target_pairs={{64,0},{72,8},{80,16},{88,24},{96,32},{104,40},{112,48},{120,56},{... | collective-permute-start | bytes 2359304 | tf_op jit(solution)/shard_map/ppermute | solution.py:17
  360.4 127.3 %collective-permute-start.3 = (bf16[1,2,256,768]{3,2,1,0:T(8,128)(2,1)}, bf16[1,2,256,768]{3,2,1,0:T(8,128)(2,1)}, u32[]{:S(2)}, u32[]{:S(2)}) collective-permute-start(bf16[1,2,256,768]{3,2,1,0:T(8,128)(2,1)} %convert_element_type.97), channel_id=1, source_target_pairs={{64,0},{72,8},{80,16},{88,24},{96,32},{104,40},{112,48},{120,56},{... | collective-permute-start | bytes 2359304 | tf_op jit(solution)/shard_map/ppermute | solution.py:17
  361.3 133.2 %collective-permute-start.4 = (bf16[1,768,256]{2,1,0:T(8,128)(2,1)}, bf16[1,768,256]{2,1,0:T(8,128)(2,1)}, u32[]{:S(2)}, u32[]{:S(2)}) collective-permute-start(bf16[1,768,256]{2,1,0:T(8,128)(2,1)} %convert_element_type.101), channel_id=1, source_target_pairs={{64,0},{72,8},{80,16},{88,24},{96,32},{104,40},{112,48},{120,56},{... | collective-permute-start | bytes 1179656 | tf_op jit(solution)/shard_map/ppermute | solution.py:17
  365.0 129.6 %collective-permute-start.5 = (bf16[1,768,256]{2,1,0:T(8,128)(2,1)}, bf16[1,768,256]{2,1,0:T(8,128)(2,1)}, u32[]{:S(2)}, u32[]{:S(2)}) collective-permute-start(bf16[1,768,256]{2,1,0:T(8,128)(2,1)} %convert_element_type.103), channel_id=1, source_target_pairs={{64,0},{72,8},{80,16},{88,24},{96,32},{104,40},{112,48},{120,56},{... | collective-permute-start | bytes 1179656 | tf_op jit(solution)/shard_map/ppermute | solution.py:17
  395.9 7.7 %copy-start.2 = (bf16[512,2048]{1,0:T(8,128)(2,1)S(1)}, bf16[512,2048]{1,0:T(8,128)(2,1)}, u32[]{:S(2)}) copy-start(bf16[512,2048]{1,0:T(8,128)(2,1)} %gather_fusion.3) | copy-start | bytes 6291460
  487.7 6.9 %copy-start.8 = (bf16[1,768,256]{2,1,0:T(8,128)(2,1)S(1)}, bf16[1,768,256]{2,1,0:T(8,128)(2,1)}, u32[]{:S(2)}) copy-start(bf16[1,768,256]{2,1,0:T(8,128)(2,1)} %broadcast_select_fusion.2) | copy-start | bytes 1179652
  487.7 6.9 %copy-start.13 = (f32[1,768,256]{2,1,0:T(8,128)S(1)}, f32[1,768,256]{2,1,0:T(8,128)}, u32[]{:S(2)}) copy-start(f32[1,768,256]{2,1,0:T(8,128)} %param.21) | copy-start | bytes 2359300
  487.7 6.9 %copy-start.15 = (f32[1,768,256]{2,1,0:T(8,128)S(1)}, f32[1,768,256]{2,1,0:T(8,128)}, u32[]{:S(2)}) copy-start(f32[1,768,256]{2,1,0:T(8,128)} %param.22) | copy-start | bytes 2359300
  489.3 8.2 %copy-start.1 = (bf16[128,2048]{1,0:T(8,128)(2,1)S(1)}, bf16[128,2048]{1,0:T(8,128)(2,1)}, u32[]{:S(2)}) copy-start(bf16[128,2048]{1,0:T(8,128)(2,1)} %param.13) | copy-start | bytes 1572868
  (7 other events, 17.3 us)
Sparse Core Ops, SparseCore 0:
  123.0 136.1 all-gather.1
  289.0 195.4 reduce-scatter.1
